TPU v7x, 256 devices: a whole 4x4x8 slice. The times are simulated.
256 devices in a mesh: outer: 8 (over y, core), inner: 32 (over x, z).
Axes of the slice: x: 4, y: 4, z: 8, core: 2. Of those that a mesh axis runs over, the one named last changes fastest.
Arguments:
- query_states: bfloat16 [65536, 4096], P(('outer', 'inner')), may hold values from -486 to 486
- key_states: bfloat16 [65536, 4096], P(('outer', 'inner')), may hold values from -18 to 18
- value_states: bfloat16 [65536, 4096], P(('outer', 'inner')), may hold values from -6 to 6
- doc_lengths: int32 [128], replicated, may hold values from 1 to 768, 65536 in all
Outputs:
- attended: bfloat16 [65536, 4096], P(('outer', 'inner'))
Inputs may be any that keep to these rules, and one draw needn't show every extreme that they name: `doc_lengths`: 128 document lengths summing to 65536; the longest is exactly 768.
All inputs are finite; a program needn't handle non-finite values.
Results may differ from a plain program's by a relative error of at most 0.0045.
Values may be sent and summed in bfloat16 or wider, within the bound.
A program may use at most 192 MiB of HBM per device.

v0:
```python
import math

import jax
import jax.numpy as jnp
from jax import lax
from jax.sharding import PartitionSpec as P

HEADS = 32
SPAN = 3


def from_behind(block, axis, distance):
    devices = range(lax.axis_size(axis))
    route = [(i - distance, i) for i in devices if i - distance in devices]
    return lax.ppermute(block, axis, route)


def doc_numbers(doc_ends, positions, token_total):
    inside = (positions >= 0) & (positions < token_total)
    counted = jnp.sum((doc_ends[None, :] <= positions[:, None]).astype(jnp.int32), axis=1)
    return jnp.where(inside, counted, -1)


def table_entry(lookup_table, entry_index):
    hits = jnp.arange(lookup_table.shape[0], dtype=jnp.int32) == entry_index
    return jnp.sum(jnp.where(hits, lookup_table, 0))


def band_attention(
    query_rows,
    query_docs,
    key_rows,
    value_rows,
    key_docs,
    first_block,
    block_count,
    block_rows,
    most_blocks,
    head_group,
):
    head_total = query_rows.shape[1]
    scaling = 1.0 / math.sqrt(query_rows.shape[2])

    def make_branch(blocks_wide):

        def attend(start_block):
            start_row = start_block * block_rows
            near_keys = lax.dynamic_slice_in_dim(key_rows, start_row, blocks_wide * block_rows, 0)
            near_values = lax.dynamic_slice_in_dim(
                value_rows, start_row, blocks_wide * block_rows, 0
            )
            near_docs = lax.dynamic_slice_in_dim(key_docs, start_row, blocks_wide * block_rows, 0)
            same_doc = (query_docs[:, None] == near_docs[None, :])[None]

            def per_group(group_index):
                query_part = lax.dynamic_slice_in_dim(
                    query_rows, group_index * head_group, head_group, 1
                )
                key_part = lax.dynamic_slice_in_dim(
                    near_keys, group_index * head_group, head_group, 1
                )
                value_part = lax.dynamic_slice_in_dim(
                    near_values, group_index * head_group, head_group, 1
                )
                scores = (
                    jnp.einsum(
                        "qhd,khd->hqk", query_part, key_part, preferred_element_type=jnp.float32
                    )
                    * scaling
                )
                masked = jnp.where(same_doc, scores, -jnp.inf)
                row_peak = jnp.max(masked, axis=2, keepdims=True)
                weights = jnp.where(same_doc, jnp.exp(masked - row_peak), 0.0)
                totals = jnp.sum(weights, axis=2)
                rounded = weights.astype(jnp.bfloat16)
                summed = jnp.einsum(
                    "hqk,khd->qhd", rounded, value_part, preferred_element_type=jnp.float32
                )
                return (summed / jnp.transpose(totals)[:, :, None]).astype(jnp.bfloat16)

            pieces = lax.map(per_group, jnp.arange(head_total // head_group, dtype=jnp.int32))
            return jnp.transpose(pieces, (1, 0, 2, 3)).reshape(query_rows.shape)

        return attend

    branches = [make_branch(blocks_wide) for blocks_wide in range(1, most_blocks + 1)]
    return lax.switch(block_count - 1, branches, first_block)


def on_device(query_states, key_states, value_states, doc_lengths):
    block_rows = query_states.shape[0]
    head_total = HEADS
    head_size = query_states.shape[1] // head_total
    token_total = block_rows * lax.axis_size(("outer", "inner"))
    doc_ends = jnp.cumsum(doc_lengths)
    doc_starts = doc_ends - doc_lengths
    query_heads = query_states.reshape(block_rows, head_total, head_size)
    block_index = lax.axis_index(("outer", "inner"))
    lower_parts = []
    upper_parts = []
    for distance in range(1, SPAN + 1):
        lower_parts.append(from_behind((key_states, value_states), ("outer", "inner"), distance))
        upper_parts.append(from_behind((key_states, value_states), ("outer", "inner"), -distance))
    ordered = lower_parts[::-1] + [(key_states, value_states)] + upper_parts
    near_keys = jnp.concatenate([member[0] for member in ordered], axis=0).reshape(
        -1, head_total, head_size
    )
    near_values = jnp.concatenate([member[1] for member in ordered], axis=0).reshape(
        -1, head_total, head_size
    )
    window_start = (block_index - SPAN) * block_rows
    key_docs = doc_numbers(
        doc_ends, window_start + jnp.arange(near_keys.shape[0], dtype=jnp.int32), token_total
    )
    query_docs = doc_numbers(
        doc_ends, block_index * block_rows + jnp.arange(block_rows, dtype=jnp.int32), token_total
    )
    first_block = table_entry(doc_starts, query_docs[0]) // block_rows - block_index + SPAN
    last_block = (table_entry(doc_ends, query_docs[-1]) - 1) // block_rows - block_index + SPAN
    result = band_attention(
        query_heads,
        query_docs,
        near_keys,
        near_values,
        key_docs,
        first_block,
        last_block - first_block + 1,
        block_rows,
        2 * SPAN + 1,
        head_total // 4,
    )
    return result.reshape(block_rows, head_total * head_size)


def solution(mesh):
    return jax.shard_map(
        on_device,
        mesh=mesh,
        in_specs=(
            P(("outer", "inner"), None),
            P(("outer", "inner"), None),
            P(("outer", "inner"), None),
            P(),
        ),
        out_specs=P(("outer", "inner"), None),
        check_vma=False,
    )
```

profile of v0, /device:TPU:20, one launch (start us, length us, event | category | flops | bytes accessed | tf_op | source)
XLA Modules:
  0.0 1062.1 jit_solution(8044784808984393288)
XLA Ops:
  0.0 6.7 collective-permute-start.6
  6.7 5.5 collective-permute-start.7
  12.2 4.1 copy.44
  22.3 3.8 collective-permute-start.8
  36.5 105.9 %collective-permute-done.6 = bf16[256,4096]{1,0:T(8,128)(2,1)} collective-permute-done((bf16[256,4096]{1,0:T(8,128)(2,1)}, bf16[256,4096]{1,0:T(8,128)(2,1)}, u32[]{:S(2)}, u32[]{:S(2)}) %collective-permute-start.6) | collective-permute-done | bytes 2097184 | tf_op jit(solution)/shard_map/ppermute | solution.py:15
  142.4 7.1 collective-permute-start.9
  152.7 85.2 %collective-permute-done.7 = bf16[256,4096]{1,0:T(8,128)(2,1)} collective-permute-done((bf16[256,4096]{1,0:T(8,128)(2,1)}, bf16[256,4096]{1,0:T(8,128)(2,1)}, u32[]{:S(2)}, u32[]{:S(2)}) %collective-permute-start.7) | collective-permute-done | bytes 2097184 | tf_op jit(solution)/shard_map/ppermute | solution.py:15
  242.9 260.8 %collective-permute-done.8 = bf16[256,4096]{1,0:T(8,128)(2,1)} collective-permute-done((bf16[256,4096]{1,0:T(8,128)(2,1)}, bf16[256,4096]{1,0:T(8,128)(2,1)}, u32[]{:S(2)}, u32[]{:S(2)}) %collective-permute-start.8) | collective-permute-done | bytes 2097184 | tf_op jit(solution)/shard_map/ppermute | solution.py:15
  503.7 5.0 collective-permute-start.11
  520.1 6.0 collective-permute-start.3
  537.2 111.0 %collective-permute-done.11 = bf16[256,4096]{1,0:T(8,128)(2,1)S(1)} collective-permute-done((bf16[256,4096]{1,0:T(8,128)(2,1)}, bf16[256,4096]{1,0:T(8,128)(2,1)S(1)}, u32[]{:S(2)}, u32[]{:S(2)}) %collective-permute-start.11) | collective-permute-done | bytes 2097184 | tf_op jit(solution)/shard_map/ppermute | solution.py:15
  649.7 18.8 %copy.51 = bf16[1792,4096]{0,1:T(8,128)(2,1)} copy(bf16[1792,4096]{1,0:T(8,128)(2,1)} %constant_dynamic-update-slice_fusion.7) | data formatting | bytes 29360128 | tf_op jit(solution)/shard_map/concatenate | solution.py:108
  674.7 15.2 %collective-permute-done.3 = bf16[256,4096]{0,1:T(8,128)(2,1)} collective-permute-done((bf16[256,4096]{0,1:T(8,128)(2,1)}, bf16[256,4096]{0,1:T(8,128)(2,1)}, u32[]{:S(2)}, u32[]{:S(2)}) %collective-permute-start.3) | collective-permute-done | bytes 2097184 | tf_op jit(solution)/shard_map/ppermute | solution.py:15
  693.0 57.7 %collective-permute-done.4 = bf16[256,4096]{0,1:T(8,128)(2,1)} collective-permute-done((bf16[256,4096]{0,1:T(8,128)(2,1)}, bf16[256,4096]{0,1:T(8,128)(2,1)}, u32[]{:S(2)}, u32[]{:S(2)}) %collective-permute-start.4) | collective-permute-done | bytes 2097184 | tf_op jit(solution)/shard_map/ppermute | solution.py:15
  753.8 163.5 %collective-permute-done.5 = bf16[256,4096]{0,1:T(8,128)(2,1)} collective-permute-done((bf16[256,4096]{0,1:T(8,128)(2,1)}, bf16[256,4096]{0,1:T(8,128)(2,1)}, u32[]{:S(2)}, u32[]{:S(2)}) %collective-permute-start.5) | collective-permute-done | bytes 2097184 | tf_op jit(solution)/shard_map/ppermute | solution.py:15
  920.6 139.7 %conditional.1 = (bf16[256,4096]{1,0:T(8,128)(2,1)S(1)}) conditional(s32[]{:T(128)} %clamp.3, (s32[]{:T(128)}, bf16[1792,32,128]{0,2,1:T(8,128)(2,1)}, bf16[1792,32,128]{0,2,1:T(8,128)(2,1)}, s32[256]{0:T(256)S(1)}, s32[1792]{0:T(1024)S(1)}, /*index=5*/bf16[256,32,128]{0,2,1:T(8,128)(2,1)S(1)}) %tuple.235, ...), branch_computations={%region_5.10_spmd, %region_10.15_spmd, %region_15.20_spmd, %region... | conditional | flops 1902053120 | bytes 205296544 | solution.py:87
  938.2 18.7 %copy.63 = bf16[1792,32,128]{2,0,1:T(8,128)(2,1)} copy(bf16[1792,32,128]{0,2,1:T(8,128)(2,1)} %get-tuple-element.620) | data formatting | bytes 29360128 | tf_op jit(solution)/shard_map
  956.9 12.1 %constant_dynamic-slice_fusion.10 = bf16[1536,32,128]{2,0,1:T(8,128)(2,1)} fusion(bf16[1792,32,128]{2,0,1:T(8,128)(2,1)} %copy.63, s32[]{:T(128)S(6)} %select_n.130), kind=kLoop, calls=%fused_computation.155 | loop fusion | bytes 25165828 | tf_op jit(solution)/shard_map/cond/branch_5_fun/dynamic_slice | solution.py:48
  970.4 5.4 constant_dynamic-slice_fusion.11
  975.9 80.1 %while.78 = (s32[]{:T(128)}, bf16[4,256,8,128]{1,3,2,0:T(8,128)(2,1)}, s32[4]{0:T(128)S(1)}, bf16[1536,32,128]{0,2,1:T(8,128)(2,1)}, bf16[256,32,128]{0,2,1:T(8,...) while((s32[]{:T(128)}, ...), condition=%wide.region_34.34_spmd.clone, body=%wide.region_31.33_spmd.clone.sunk | while | flops 1636697600 | bytes 62677736 | solution.py:81
  977.2 3.9 fusion.372
  981.4 7.6 fusion.373
  989.1 6.8 fusion.374
  997.3 3.9 fusion.372
  1001.4 7.6 fusion.373
  1009.1 6.8 fusion.374
  1017.3 3.9 fusion.372
  1021.5 7.6 fusion.373
  1029.1 6.8 fusion.374
  1037.3 3.9 fusion.372
  1041.5 7.6 fusion.373
  1049.1 6.8 fusion.374
  (71 shorter events, 70.7 us)
Async XLA Ops:
  0.0 26.1 %copy-start.4 = (s32[128]{0:T(128)S(1)}, s32[128]{0:T(128)}, u32[]{:S(2)}) copy-start(s32[128]{0:T(128)} %param.28) | copy-start | bytes 1540
  0.0 142.4 %collective-permute-start.6 = (bf16[256,4096]{1,0:T(8,128)(2,1)}, bf16[256,4096]{1,0:T(8,128)(2,1)}, u32[]{:S(2)}, u32[]{:S(2)}) collective-permute-start(bf16[256,4096]{1,0:T(8,128)(2,1)} %param.27), channel_id=1, source_target_pairs={{0,3},{1,4},{2,5},{3,6},{4,7},{5,8},{6,9},{7,10},{8,11},{9,12},{10... | collective-permute-start | bytes 6291464 | tf_op jit(solution)/shard_map/ppermute | solution.py:15
  6.7 231.2 %collective-permute-start.7 = (bf16[256,4096]{1,0:T(8,128)(2,1)}, bf16[256,4096]{1,0:T(8,128)(2,1)}, u32[]{:S(2)}, u32[]{:S(2)}) collective-permute-start(bf16[256,4096]{1,0:T(8,128)(2,1)} %param.27), channel_id=1, source_target_pairs={{0,2},{1,3},{2,4},{3,5},{4,6},{5,7},{6,8},{7,9},{8,10},{9,11},{10,... | collective-permute-start | bytes 6291464 | tf_op jit(solution)/shard_map/ppermute | solution.py:15
  16.2 498.8 %collective-permute-start = (bf16[256,4096]{0,1:T(8,128)(2,1)}, bf16[256,4096]{0,1:T(8,128)(2,1)}, u32[]{:S(2)}, u32[]{:S(2)}) collective-permute-start(bf16[256,4096]{0,1:T(8,128)(2,1)} %copy.44), channel_id=1, source_target_pairs={{0,3},{1,4},{2,5},{3,6},{4,7},{5,8},{6,9},{7,10},{8,11},{9,12},{10... | collective-permute-start | bytes 6291464 | tf_op jit(solution)/shard_map/ppermute | solution.py:15
  18.6 501.5 %collective-permute-start.1 = (bf16[256,4096]{0,1:T(8,128)(2,1)}, bf16[256,4096]{0,1:T(8,128)(2,1)}, u32[]{:S(2)}, u32[]{:S(2)}) collective-permute-start(bf16[256,4096]{0,1:T(8,128)(2,1)} %copy.44), channel_id=1, source_target_pairs={{0,2},{1,3},{2,4},{3,5},{4,6},{5,7},{6,8},{7,9},{8,10},{9,11},{10,... | collective-permute-start | bytes 6291464 | tf_op jit(solution)/shard_map/ppermute | solution.py:15
  22.3 481.4 %collective-permute-start.8 = (bf16[256,4096]{1,0:T(8,128)(2,1)}, bf16[256,4096]{1,0:T(8,128)(2,1)}, u32[]{:S(2)}, u32[]{:S(2)}) collective-permute-start(bf16[256,4096]{1,0:T(8,128)(2,1)} %param.27), channel_id=1, source_target_pairs={{0,1},{1,2},{2,3},{3,4},{4,5},{5,6},{6,7},{7,8},{8,9},{9,10},{10,1... | collective-permute-start | bytes 6291464 | tf_op jit(solution)/shard_map/ppermute | solution.py:15
  142.4 386.9 %collective-permute-start.9 = (bf16[256,4096]{1,0:T(8,128)(2,1)}, bf16[256,4096]{1,0:T(8,128)(2,1)S(1)}, u32[]{:S(2)}, u32[]{:S(2)}) collective-permute-start(bf16[256,4096]{1,0:T(8,128)(2,1)} %param.27), channel_id=1, source_target_pairs={{1,0},{2,1},{3,2},{4,3},{5,4},{6,5},{7,6},{8,7},{9,8},{10,9},{11,1... | collective-permute-start | bytes 6291464 | tf_op jit(solution)/shard_map/ppermute | solution.py:15
  237.9 294.8 %collective-permute-start.10 = (bf16[256,4096]{1,0:T(8,128)(2,1)}, bf16[256,4096]{1,0:T(8,128)(2,1)S(1)}, u32[]{:S(2)}, u32[]{:S(2)}) collective-permute-start(bf16[256,4096]{1,0:T(8,128)(2,1)} %param.27), channel_id=1, source_target_pairs={{2,0},{3,1},{4,2},{5,3},{6,4},{7,5},{8,6},{9,7},{10,8},{11,9},{12,... | collective-permute-start | bytes 6291464 | tf_op jit(solution)/shard_map/ppermute | solution.py:15
  503.7 144.5 %collective-permute-start.11 = (bf16[256,4096]{1,0:T(8,128)(2,1)}, bf16[256,4096]{1,0:T(8,128)(2,1)S(1)}, u32[]{:S(2)}, u32[]{:S(2)}) collective-permute-start(bf16[256,4096]{1,0:T(8,128)(2,1)} %param.27), channel_id=1, source_target_pairs={{3,0},{4,1},{5,2},{6,3},{7,4},{8,5},{9,6},{10,7},{11,8},{12,9},{13... | collective-permute-start | bytes 6291464 | tf_op jit(solution)/shard_map/ppermute | solution.py:15
  515.0 153.4 %collective-permute-start.2 = (bf16[256,4096]{0,1:T(8,128)(2,1)}, bf16[256,4096]{0,1:T(8,128)(2,1)}, u32[]{:S(2)}, u32[]{:S(2)}) collective-permute-start(bf16[256,4096]{0,1:T(8,128)(2,1)} %copy.44), channel_id=1, source_target_pairs={{0,1},{1,2},{2,3},{3,4},{4,5},{5,6},{6,7},{7,8},{8,9},{9,10},{10,1... | collective-permute-start | bytes 6291464 | tf_op jit(solution)/shard_map/ppermute | solution.py:15
  520.1 169.8 %collective-permute-start.3 = (bf16[256,4096]{0,1:T(8,128)(2,1)}, bf16[256,4096]{0,1:T(8,128)(2,1)}, u32[]{:S(2)}, u32[]{:S(2)}) collective-permute-start(bf16[256,4096]{0,1:T(8,128)(2,1)} %copy.44), channel_id=1, source_target_pairs={{1,0},{2,1},{3,2},{4,3},{5,4},{6,5},{7,6},{8,7},{9,8},{10,9},{11,1... | collective-permute-start | bytes 6291464 | tf_op jit(solution)/shard_map/ppermute | solution.py:15
  529.3 221.5 %collective-permute-start.4 = (bf16[256,4096]{0,1:T(8,128)(2,1)}, bf16[256,4096]{0,1:T(8,128)(2,1)}, u32[]{:S(2)}, u32[]{:S(2)}) collective-permute-start(bf16[256,4096]{0,1:T(8,128)(2,1)} %copy.44), channel_id=1, source_target_pairs={{2,0},{3,1},{4,2},{5,3},{6,4},{7,5},{8,6},{9,7},{10,8},{11,9},{12,... | collective-permute-start | bytes 6291464 | tf_op jit(solution)/shard_map/ppermute | solution.py:15
  532.6 384.8 %collective-permute-start.5 = (bf16[256,4096]{0,1:T(8,128)(2,1)}, bf16[256,4096]{0,1:T(8,128)(2,1)}, u32[]{:S(2)}, u32[]{:S(2)}) collective-permute-start(bf16[256,4096]{0,1:T(8,128)(2,1)} %copy.44), channel_id=1, source_target_pairs={{3,0},{4,1},{5,2},{6,3},{7,4},{8,5},{9,6},{10,7},{11,8},{12,9},{13... | collective-permute-start | bytes 6291464 | tf_op jit(solution)/shard_map/ppermute | solution.py:15
  956.9 13.5 %copy-start = (bf16[1792,32,128]{0,2,1:T(8,128)(2,1)S(1)}, bf16[1792,32,128]{0,2,1:T(8,128)(2,1)}, u32[]{:S(2)}) copy-start(bf16[1792,32,128]{0,2,1:T(8,128)(2,1)} %get-tuple-element.386) | copy-start | bytes 44040196 | tf_op jit(solution)/shard_map/cond
  975.9 1.4 copy-start.1
  989.1 6.8 copy-start.2
  995.9 1.4 copy-start.1
  1009.1 6.8 copy-start.2
  1015.9 1.4 copy-start.1
  1029.1 6.8 copy-start.2
  1035.9 1.4 copy-start.1
  1049.1 6.8 copy-start.2
  1060.2 1.3 copy-start.3
where the time goes:
time: 1070 us; the launch traced here: 1060 us
  waiting for transfers between devices  799 us (75%)
  local copies, waits for them, and re-layouts  111 us (10%)
  starting transfers between devices  49 us (5%)
  matrix products  42.9 us (4%)
  other arithmetic  34.7 us (3%)
  loops' own time  21.4 us (2%)
    ppermute x12, waiting for transfers between devices, from_behind(): return lax.ppermute(block, axis, route)  799 us
    ppermute x12, starting transfers between devices, from_behind(): return lax.ppermute(block, axis, route)  49 us
    unnamed x18, local copies, waits for them, and re-layouts  42.9 us
    sub x4, other arithmetic, per_group(): weights = jnp.where(same_doc, jnp.exp(masked - row_peak), 0.0)  30.6 us
    dot_general x4, matrix products, per_group(): jnp.einsum('hqk,khd->qhd', rounded, value_part, preferred_element_type=jn...  27.3 us
  transfers between devices with their start and end apart: 12, of which 7 were waited for; matrix products, arithmetic and copies ran while one was open for 6% of the time, Pallas kernels for 0%

commit v1 on v0

v1 whole, which is shorter than its diff:
```python
import functools
import math

import jax
import jax.numpy as jnp
from jax import lax
from jax.experimental import pallas as pl
from jax.experimental.pallas import tpu as pltpu
from jax.sharding import PartitionSpec as P

HEADS = 32
SPAN = 3
RING = 8
MESH = pl.DeviceIdType.MESH
MASKED = -1e30


def kernel(
    outer_size,
    inner_size,
    lengths_ref,
    query_ref,
    key_ref,
    value_ref,
    out_ref,
    keys,
    values,
    queries,
    results,
    doc_rows,
    doc_cols,
    key_send,
    key_recv,
    value_send,
    value_recv,
    query_send,
    query_recv,
    result_send,
    result_recv,
    halo_send,
    halo_recv,
    own_sem,
):
    rows = query_ref.shape[0]
    size = keys.shape[2]
    own_heads = keys.shape[0]
    group_cols = own_heads * size
    halo_rows = SPAN * rows
    doc_total = lengths_ref.shape[0]
    blocks = outer_size * inner_size
    outer = lax.axis_index("outer")
    inner = lax.axis_index("inner")
    place = lax.rem(inner, RING)
    line_start = inner - place
    block_index = outer * inner_size + inner

    def ring_device(other):
        return (outer, line_start + other)

    def group_device(step):
        other = lax.rem(block_index + step * RING + blocks, blocks)
        return (lax.div(other, inner_size), lax.rem(other, inner_size))

    def ring_place(offset):
        return lax.rem(place + offset, RING)

    def columns(owner, head):
        return pl.ds(pl.multiple_of(owner * group_cols + head * size, size), size)

    def key_slot(head, source):
        return keys.at[head, pl.ds(pl.multiple_of(halo_rows + source * rows, rows), rows), :]

    def value_slot(head, source):
        return values.at[head, pl.ds(pl.multiple_of(halo_rows + source * rows, rows), rows), :]

    def query_slot(head, source):
        return queries.at[head, pl.ds(pl.multiple_of(source * rows, rows), rows), :]

    def result_slot(head, target):
        return results.at[head, pl.ds(pl.multiple_of(target * rows, rows), rows), :]

    streams = {
        "key": (key_ref, key_slot, key_send, key_recv),
        "value": (value_ref, value_slot, value_send, value_recv),
        "query": (query_ref, query_slot, query_send, query_recv),
    }

    def ring_copy(kind, head, offset):
        source, slot, send, recv = streams[kind]
        owner = ring_place(offset)
        return pltpu.make_async_remote_copy(
            src_ref=source.at[:, columns(owner, head)],
            dst_ref=slot(head, place),
            send_sem=send.at[head, owner],
            recv_sem=recv.at[head, place],
            device_id=ring_device(owner),
            device_id_type=MESH,
        )

    def ring_arrival(kind, head, offset):
        source, slot, send, recv = streams[kind]
        other = ring_place(offset)
        return pltpu.make_async_remote_copy(
            src_ref=source.at[:, columns(other, head)],
            dst_ref=slot(head, other),
            send_sem=send.at[head, other],
            recv_sem=recv.at[head, other],
            device_id=ring_device(other),
            device_id_type=MESH,
        )

    def own_copy(kind, head):
        source, slot, send, recv = streams[kind]
        return pltpu.make_async_copy(
            source.at[:, columns(place, head)], slot(head, place), recv.at[head, place]
        )

    def halo_copy(which, head, up):
        buffer = (keys, values)[which]
        edge = halo_rows + RING * rows
        source_row = edge - halo_rows if up else halo_rows
        target_row = 0 if up else edge
        return pltpu.make_async_remote_copy(
            src_ref=buffer.at[head, pl.ds(source_row, halo_rows), :],
            dst_ref=buffer.at[head, pl.ds(target_row, halo_rows), :],
            send_sem=halo_send.at[head, which, 0 if up else 1],
            recv_sem=halo_recv.at[head, which, 0 if up else 1],
            device_id=group_device(1 if up else -1),
            device_id_type=MESH,
        )

    def result_copy(head, target):
        return pltpu.make_async_remote_copy(
            src_ref=result_slot(head, target),
            dst_ref=out_ref.at[:, columns(place, head)],
            send_sem=result_send.at[head, target],
            recv_sem=result_recv.at[head, place],
            device_id=ring_device(target),
            device_id_type=MESH,
        )

    def result_arrival(head, source):
        return pltpu.make_async_remote_copy(
            src_ref=result_slot(head, source),
            dst_ref=out_ref.at[:, columns(source, head)],
            send_sem=result_send.at[head, source],
            recv_sem=result_recv.at[head, source],
            device_id=ring_device(source),
            device_id_type=MESH,
        )

    barrier = pltpu.get_barrier_semaphore()
    for offset in range(1, RING):
        pl.semaphore_signal(
            barrier, inc=1, device_id=ring_device(ring_place(offset)), device_id_type=MESH
        )
    for step in (1, -1):
        pl.semaphore_signal(
            barrier, inc=1, device_id=group_device(step), device_id_type=MESH
        )
    pl.semaphore_wait(barrier, RING + 1)

    order = (1, 7, 2, 6, 3, 5, 4)

    @pl.loop(0, own_heads)
    def _(head):
        for kind in ("key", "value", "query"):
            own_copy(kind, head).start()
            for offset in order:
                ring_copy(kind, head, offset).start()

    window = 2 * SPAN + RING
    first_position = (block_index - place - SPAN) * rows
    positions = (
        first_position
        + lax.broadcasted_iota(jnp.int32, doc_rows.shape, 0) * rows
        + lax.broadcasted_iota(jnp.int32, doc_rows.shape, 1)
    )

    def count(doc, carry):
        end, counted = carry
        end = end + lengths_ref[doc]
        return end, counted + jnp.where(positions >= end, 1, 0)

    _, counted = lax.fori_loop(0, doc_total, count, (jnp.int32(0), jnp.zeros_like(positions)))
    inside = (positions >= 0) & (positions < blocks * rows)
    doc_rows[...] = jnp.where(inside, counted, -1).astype(jnp.float32)
    for block in range(RING):
        row = doc_rows[SPAN + block : SPAN + block + 1, :]
        doc_cols[block * rows : (block + 1) * rows, :] = jnp.transpose(
            jnp.broadcast_to(row, (rows, rows))
        )

    scaling = 1.0 / math.sqrt(size)

    def attend(head, block):
        start = pl.multiple_of(block * rows, rows)
        query = queries[head, pl.ds(start, rows), :]
        query_docs = doc_cols[pl.ds(start, rows), :]
        scores = []
        peak = None
        for step in range(2 * SPAN + 1):
            key = keys[head, pl.ds(start + step * rows, rows), :]
            key_docs = doc_rows[pl.ds(block + step, 1), :]
            raw = lax.dot_general(
                query, key, (((1,), (1,)), ((), ())), preferred_element_type=jnp.float32
            )
            masked = jnp.where(query_docs == key_docs, raw * scaling, MASKED)
            scores.append(masked)
            peak = masked if peak is None else jnp.maximum(peak, masked)
        peak = jnp.max(peak, axis=1, keepdims=True)
        totals = None
        summed = None
        for step in range(2 * SPAN + 1):
            value = values[head, pl.ds(start + step * rows, rows), :]
            weights = jnp.exp(scores[step] - peak)
            part = jnp.dot(
                weights.astype(jnp.bfloat16), value, preferred_element_type=jnp.float32
            )
            totals = weights if totals is None else totals + weights
            summed = part if summed is None else summed + part
        totals = jnp.sum(totals, axis=1, keepdims=True)
        results[head, pl.ds(start, rows), :] = (summed / totals).astype(jnp.bfloat16)

    def gather(head):
        for kind in ("key", "value"):
            own_copy(kind, head).wait()
            for offset in order:
                ring_arrival(kind, head, offset).wait_recv()
        for up in (True, False):
            for which in (0, 1):
                halo_copy(which, head, up).start()

    def compute(head):
        own_copy("query", head).wait()
        for offset in order:
            ring_arrival("query", head, offset).wait_recv()
        for up in (True, False):
            for which in (0, 1):
                halo_copy(which, head, up).wait_recv()

        @pl.loop(1, RING)
        def _(offset):
            target = ring_place(offset)
            attend(head, target)
            result_copy(head, target).start()

        attend(head, place)
        pltpu.make_async_copy(
            result_slot(head, place), out_ref.at[:, columns(place, head)], own_sem.at[head]
        ).start()

    gather(0)

    @pl.loop(0, own_heads - 1)
    def _(head):
        gather(head + 1)
        compute(head)

    compute(own_heads - 1)

    @pl.loop(0, own_heads)
    def _(head):
        pltpu.make_async_copy(
            result_slot(head, place), out_ref.at[:, columns(place, head)], own_sem.at[head]
        ).wait()
        for offset in order:
            result_arrival(head, ring_place(offset)).wait_recv()
            for kind in ("key", "value", "query"):
                ring_copy(kind, head, offset).wait_send()
            result_copy(head, ring_place(offset)).wait_send()
        for up in (True, False):
            for which in (0, 1):
                halo_copy(which, head, up).wait_send()


def on_device(query_states, key_states, value_states, doc_lengths):
    rows, width = query_states.shape
    outer_size = lax.axis_size("outer")
    inner_size = lax.axis_size("inner")
    size = width // HEADS
    own_heads = HEADS // RING
    window_rows = (RING + 2 * SPAN) * rows
    pair_sems = pltpu.SemaphoreType.DMA((own_heads, RING))
    hbm = pl.BlockSpec(memory_space=pl.ANY)
    return pl.pallas_call(
        functools.partial(kernel, outer_size, inner_size),
        out_shape=jax.ShapeDtypeStruct((rows, width), jnp.bfloat16),
        in_specs=[pl.BlockSpec(memory_space=pltpu.SMEM), hbm, hbm, hbm],
        out_specs=hbm,
        scratch_shapes=[
            pltpu.VMEM((own_heads, window_rows, size), jnp.bfloat16),
            pltpu.VMEM((own_heads, window_rows, size), jnp.bfloat16),
            pltpu.VMEM((own_heads, RING * rows, size), jnp.bfloat16),
            pltpu.VMEM((own_heads, RING * rows, size), jnp.bfloat16),
            pltpu.VMEM((16, rows), jnp.float32),
            pltpu.VMEM((RING * rows, rows), jnp.float32),
        ]
        + [pair_sems] * 8
        + [
            pltpu.SemaphoreType.DMA((own_heads, 2, 2)),
            pltpu.SemaphoreType.DMA((own_heads, 2, 2)),
            pltpu.SemaphoreType.DMA((own_heads,)),
        ],
        name="ring_heads_attention",
        compiler_params=pltpu.CompilerParams(
            collective_id=0, has_side_effects=True, vmem_limit_bytes=48 * 1024 * 1024
        ),
    )(doc_lengths, query_states, key_states, value_states)


def solution(mesh):
    return jax.shard_map(
        on_device,
        mesh=mesh,
        in_specs=(
            P(("outer", "inner"), None),
            P(("outer", "inner"), None),
            P(("outer", "inner"), None),
            P(),
        ),
        out_specs=P(("outer", "inner"), None),
        check_vma=False,
    )
```

time: 1070 us -> 197 us (0.18)
  the two profiles are of different devices: /device:TPU:20 before, /device:TPU:0 now
where the time goes in v1:
time: 197 us; the launch traced here: 195 us
  Pallas kernels  191 us (97%)
  local copies, waits for them, and re-layouts  3.57 us (2%)
    pallas_call x1, Pallas kernels, on_device(): pl.pallas_call(functools.partial(kernel, outer_size, inner_size), out_sha...  191 us

profile of v1, /device:TPU:0, one launch (start us, length us, event | category | flops | bytes accessed | tf_op | source)
XLA Modules:
  0.0 194.9 jit_solution(10045456742368577752)
XLA Ops:
  0.0 0.0 copy-start
  0.0 1.6 copy-done
  1.6 0.0 copy-start.1
  1.6 0.7 copy-done.1
  2.2 191.3 %ring_heads_attention.1 = bf16[256,4096]{1,0:T(8,128)(2,1)S(1)} custom-call(s32[128]{0:T(128)S(1)} %copy-done.1, bf16[256,4096]{1,0:T(8,128)(2,1)S(1)} %copy-done, bf16[256,4096]{1,0:T(8,128)(2,1)} %key_ref.1, bf16[256,4096]{1,0:T(8,128)(2,1)} %value_ref.1), custom_call_target="tpu_custom_call" | custom-call | tf_op jit(solution)/shard_map/ring_heads_attention/pallas_call | solution.py:286
  193.5 1.3 copy.6
Async XLA Ops:
  0.0 1.6 copy-start
  1.6 0.7 copy-start.1

commit v2 on v0

v2 whole, which is shorter than its diff:
```python
import functools
import math

import jax
import jax.numpy as jnp
from jax import lax
from jax.experimental import pallas as pl
from jax.experimental.pallas import tpu as pltpu
from jax.sharding import PartitionSpec as P

HEADS = 32
SPAN = 3
MESH = pl.DeviceIdType.MESH
MASKED = -1e30
LANES = 128
SUBLANES = 8


def pack_column(column):
    groups = column.shape[0] // SUBLANES
    shape = (SUBLANES, LANES)
    lane = lax.broadcasted_iota(jnp.int32, shape, 1)
    lane_in_group = lane % groups
    tile = jnp.broadcast_to(column[:SUBLANES], shape)
    for group in range(1, groups):
        part = column[group * SUBLANES : (group + 1) * SUBLANES]
        tile = jnp.where(lane_in_group == group, jnp.broadcast_to(part, shape), tile)
    folded = tile
    for pair in range(1, LANES // groups):
        shifted = pltpu.roll(tile, SUBLANES - 2 * pair, axis=0)
        folded = jnp.where(lane // groups == pair, shifted, folded)
    return folded[:2]


def unpack_column(packed, rows):
    groups = rows // SUBLANES
    shape = (SUBLANES, LANES)
    sublane = lax.broadcasted_iota(jnp.int32, shape, 0)
    stacked = jnp.concatenate([packed] * (SUBLANES // 2), axis=0)
    tile = stacked
    for pair in range(1, LANES // groups):
        shifted = pltpu.roll(stacked, LANES - groups * pair, axis=1)
        tile = jnp.where(sublane // 2 == pair, shifted, tile)
    return jnp.concatenate(
        [jnp.broadcast_to(tile[:, group : group + 1], shape) for group in range(groups)], axis=0
    )


def kernel(
    outer_size,
    inner_size,
    lengths_ref,
    query_ref,
    key_ref,
    value_ref,
    out_ref,
    queries,
    keys,
    values,
    results,
    in_data,
    in_stat,
    out_data,
    out_stat,
    bias,
    doc_rows,
    doc_cols,
    select,
    load_sem,
    store_sem,
    data_send,
    data_recv,
    stat_send,
    stat_recv,
):
    heads, rows, size = queries.shape
    slots = in_data.shape[2]
    doc_total = lengths_ref.shape[0]
    blocks = outer_size * inner_size
    outer = lax.axis_index("outer")
    inner = lax.axis_index("inner")
    block_index = outer * inner_size + inner
    scaling = 1.0 / math.sqrt(size)

    def device_of(block):
        wrapped = lax.rem(block + blocks, blocks)
        return (lax.div(wrapped, inner_size), lax.rem(wrapped, inner_size))

    neighbours = (device_of(block_index + 1), device_of(block_index - 1))

    barrier = pltpu.get_barrier_semaphore()
    for neighbour in neighbours:
        pl.semaphore_signal(barrier, inc=1, device_id=neighbour, device_id_type=MESH)

    def load(which, head):
        source = (query_ref, key_ref, value_ref)[which]
        target = (queries, keys, values)[which]
        columns = pl.ds(pl.multiple_of(head * size, size), size)
        return pltpu.make_async_copy(
            source.at[:, columns], target.at[head], load_sem.at[which, head]
        )

    def store(head):
        columns = pl.ds(pl.multiple_of(head * size, size), size)
        return pltpu.make_async_copy(
            results.at[head], out_ref.at[:, columns], store_sem.at[head]
        )

    @pl.loop(0, heads)
    def _(head):
        for which in range(3):
            load(which, head).start()

    positions = (
        (block_index - SPAN) * rows
        + lax.broadcasted_iota(jnp.int32, doc_rows.shape, 0) * rows
        + lax.broadcasted_iota(jnp.int32, doc_rows.shape, 1)
    )

    def count(doc, carry):
        end, counted = carry
        end = end + lengths_ref[doc]
        return end, counted + jnp.where(positions >= end, 1, 0)

    _, counted = lax.fori_loop(0, doc_total, count, (jnp.int32(0), jnp.zeros_like(positions)))
    inside = (positions >= 0) & (positions < blocks * rows)
    doc_rows[...] = jnp.where(inside, counted, -1).astype(jnp.float32)
    for block in range(2 * SPAN + 1):
        row = doc_rows[block : block + 1, :]
        column = jnp.transpose(jnp.broadcast_to(row, (LANES, rows)))
        doc_cols[block] = column
        for half in range(rows // LANES):
            lanes = slice(half * LANES, (half + 1) * LANES)
            key_docs = doc_rows[SPAN : SPAN + 1, lanes]
            bias[block, :, lanes] = jnp.where(column == key_docs, 0.0, MASKED)
    edges = (doc_rows[SPAN + 1 : SPAN + 2, 0:1], doc_rows[SPAN - 1 : SPAN, rows - 1 : rows])
    for way in range(2):
        sign = 1 - 2 * way
        for hop in range(SPAN):
            select[way, hop] = jnp.where(
                doc_cols[SPAN - sign * hop] == edges[way], 1.0, 0.0
            )

    pl.semaphore_wait(barrier, 2)

    def send(way, hop, slot):
        data = pltpu.make_async_remote_copy(
            src_ref=out_data.at[way, hop, slot],
            dst_ref=in_data.at[way, hop, slot],
            send_sem=data_send.at[way, hop, slot],
            recv_sem=data_recv.at[way, hop, slot],
            device_id=neighbours[way],
            device_id_type=MESH,
        )
        stat = pltpu.make_async_remote_copy(
            src_ref=out_stat.at[way, hop, slot, pl.ds(0, 2), :],
            dst_ref=in_stat.at[way, hop, slot, pl.ds(0, 2), :],
            send_sem=stat_send.at[way, hop, slot],
            recv_sem=stat_recv.at[way, hop, slot],
            device_id=neighbours[way],
            device_id_type=MESH,
        )
        return stat, data

    def arrive(way, hop, slot):
        for copy in send(way, hop, slot):
            copy.wait_recv()

    def attend(query, head, offset):
        raw = lax.dot_general(
            query, keys[head], (((1,), (1,)), ((), ())), preferred_element_type=jnp.float32
        )
        scores = raw * scaling + bias[SPAN + offset]
        peak = jnp.max(scores, axis=1, keepdims=True)
        weights = jnp.exp(scores - peak)
        total = jnp.sum(weights, axis=1, keepdims=True)
        summed = jnp.dot(
            weights.astype(jnp.bfloat16), values[head], preferred_element_type=jnp.float32
        )
        return summed, peak, total

    def arrived(way, hop, slot):
        data = in_data[way, hop, slot].astype(jnp.float32)
        return data, unpack_column(in_stat[way, hop, slot, 0:2, :], rows)[:, :1]

    def merge(partial, others):
        summed, peak, total = partial
        top = peak
        for _, level in others:
            top = jnp.maximum(top, level)
        own = jnp.exp(peak - top)
        summed = summed * own
        total = total * own
        for data, level in others:
            share = jnp.exp(level - top)
            summed = summed + data * share
            total = total + share
        return summed / total, top + jnp.log(total)

    def put(way, hop, slot, query, output, level):
        taken = select[way, hop] > 0.5
        out_data[way, hop, slot] = jnp.where(
            taken, query.astype(jnp.float32), output
        ).astype(jnp.bfloat16)
        out_stat[way, hop, slot, 0:2, :] = pack_column(
            jnp.where(taken[:, :1], MASKED, level)
        )
        for copy in send(way, hop, slot):
            copy.start()

    def pass_on(step, hop):
        slot = step - hop
        for way in range(2):
            sign = 1 - 2 * way
            if hop == 0:
                query = queries[jnp.minimum(step, heads - 1)]
            else:
                query = in_data[way, hop - 1, slot]
            head = step - SPAN - 1 - hop

            @pl.when(head >= 0)
            def _():
                back = in_data[1 - way, SPAN - 1 - hop, head]
                partial = attend(back, head, sign * (SPAN - hop))
                others = [arrived(way, hop - 1, slot)] if hop else []
                output, level = merge(partial, others)
                put(way, hop, slot, query, output, level)

            @pl.when(head < 0)
            def _():
                put(
                    way,
                    hop,
                    slot,
                    query,
                    jnp.zeros((rows, size), jnp.float32),
                    jnp.full((rows, 1), MASKED, jnp.float32),
                )

    last = slots + SPAN

    @pl.loop(0, last + 1)
    def _(step):
        @pl.when(step < heads)
        def _():
            load(0, step).wait()

        @pl.when((step >= SPAN + 1) & (step < SPAN + 1 + heads))
        def _():
            for which in (1, 2):
                load(which, step - SPAN - 1).wait()

        @pl.when(step >= SPAN + 1)
        def _():
            for way in range(2):
                arrive(way, SPAN - 1, step - SPAN - 1)

        for hop in range(SPAN):

            @pl.when((step >= hop) & (step < slots + hop))
            def _():
                if hop:
                    for way in range(2):
                        arrive(way, hop - 1, step - hop)
                pass_on(step, hop)

        @pl.when(step >= 2 * SPAN + 2)
        def _():
            head = step - 2 * SPAN - 2
            partial = attend(queries[head], head, 0)
            others = [arrived(way, SPAN - 1, step - SPAN - 1) for way in range(2)]
            output, _ = merge(partial, others)
            results[head] = output.astype(jnp.bfloat16)
            store(head).start()

    @pl.loop(0, heads)
    def _(head):
        store(head).wait()

    @pl.loop(0, slots)
    def _(slot):
        for way in range(2):
            for hop in range(SPAN):
                for copy in send(way, hop, slot):
                    copy.wait_send()


def on_device(query_states, key_states, value_states, doc_lengths):
    rows, width = query_states.shape
    size = width // HEADS
    slots = HEADS + SPAN + 1
    hbm = pl.BlockSpec(memory_space=pl.ANY)
    mail = pltpu.VMEM((2, SPAN, slots, rows, size), jnp.bfloat16)
    stats = pltpu.VMEM((2, SPAN, slots, SUBLANES, LANES), jnp.float32)
    held = pltpu.VMEM((HEADS, rows, size), jnp.bfloat16)
    mail_sems = pltpu.SemaphoreType.DMA((2, SPAN, slots))
    return pl.pallas_call(
        functools.partial(kernel, lax.axis_size("outer"), lax.axis_size("inner")),
        out_shape=jax.ShapeDtypeStruct((rows, width), jnp.bfloat16),
        in_specs=[pl.BlockSpec(memory_space=pltpu.SMEM), hbm, hbm, hbm],
        out_specs=hbm,
        scratch_shapes=[
            held,
            held,
            held,
            held,
            mail,
            stats,
            mail,
            stats,
            pltpu.VMEM((2 * SPAN + 1, rows, rows), jnp.float32),
            pltpu.VMEM((SUBLANES, rows), jnp.float32),
            pltpu.VMEM((2 * SPAN + 1, rows, LANES), jnp.float32),
            pltpu.VMEM((2, SPAN, rows, LANES), jnp.float32),
            pltpu.SemaphoreType.DMA((3, HEADS)),
            pltpu.SemaphoreType.DMA((HEADS,)),
            mail_sems,
            mail_sems,
            mail_sems,
            mail_sems,
        ],
        name="query_mail_attention",
        compiler_params=pltpu.CompilerParams(
            collective_id=0, has_side_effects=True, vmem_limit_bytes=56 * 1024 * 1024
        ),
    )(doc_lengths, query_states, key_states, value_states)


def solution(mesh):
    return jax.shard_map(
        on_device,
        mesh=mesh,
        in_specs=(
            P(("outer", "inner"), None),
            P(("outer", "inner"), None),
            P(("outer", "inner"), None),
            P(),
        ),
        out_specs=P(("outer", "inner"), None),
        check_vma=False,
    )
```

time: 1070 us -> 231 us (0.22)
  the two profiles are of different devices: /device:TPU:20 before, /device:TPU:0 now
where the time goes in v2:
time: 231 us; the launch traced here: 230 us
  Pallas kernels  227 us (98%)
  local copies, waits for them, and re-layouts  3.13 us (1%)
    pallas_call x1, Pallas kernels, on_device(): pl.pallas_call(functools.partial(kernel, lax.axis_size('outer'), lax.axis...  227 us

profile of v2, /device:TPU:0, one launch (start us, length us, event | category | flops | bytes accessed | tf_op | source)
XLA Modules:
  0.0 230.4 jit_solution(3902398845769218401)
XLA Ops:
  0.0 227.3 %query_mail_attention.1 = bf16[256,4096]{1,0:T(8,128)(2,1)} custom-call(s32[128]{0:T(128)} %lengths_ref.1, bf16[256,4096]{1,0:T(8,128)(2,1)} %query_ref.1, bf16[256,4096]{1,0:T(8,128)(2,1)} %key_ref.1, bf16[256,4096]{1,0:T(8,128)(2,1)} %value_ref.1), custom_call_target="tpu_custom_call" | custom-call | tf_op jit(solution)/shard_map/query_mail_attention/pallas_call | solution.py:297
  227.3 3.1 %copy.6 = bf16[256,4096]{1,0:T(8,128)(2,1)} copy(bf16[256,4096]{1,0:T(8,128)(2,1)} %query_mail_attention.1) | data formatting | bytes 4194304

commit v3 on v2

v3 whole, which is shorter than its diff:
```python
import functools
import math

import jax
import jax.numpy as jnp
from jax import lax
from jax.experimental import pallas as pl
from jax.experimental.pallas import tpu as pltpu
from jax.sharding import PartitionSpec as P

HEADS = 32
SPAN = 3
MESH = pl.DeviceIdType.MESH
MASKED = -1e30
LANES = 128
SUBLANES = 8


def flip(block):
    return jnp.transpose(block.astype(jnp.float32)).astype(jnp.bfloat16)


def kernel(
    outer_size,
    inner_size,
    lengths_ref,
    query_ref,
    key_ref,
    value_ref,
    out_ref,
    queries,
    keys,
    values,
    results,
    in_data,
    in_stat,
    out_data,
    out_stat,
    bias,
    doc_rows,
    select,
    queries_t,
    values_t,
    load_sem,
    store_sem,
    data_send,
    data_recv,
    stat_send,
    stat_recv,
):
    heads, rows, size = queries.shape
    slots = in_data.shape[2]
    doc_total = lengths_ref.shape[0]
    blocks = outer_size * inner_size
    outer = lax.axis_index("outer")
    inner = lax.axis_index("inner")
    block_index = outer * inner_size + inner
    scaling = 1.0 / math.sqrt(size)

    def device_of(block):
        wrapped = lax.rem(block + blocks, blocks)
        return (lax.div(wrapped, inner_size), lax.rem(wrapped, inner_size))

    neighbours = (device_of(block_index + 1), device_of(block_index - 1))

    barrier = pltpu.get_barrier_semaphore()
    for neighbour in neighbours:
        pl.semaphore_signal(barrier, inc=1, device_id=neighbour, device_id_type=MESH)

    def load(which, head):
        source = (query_ref, key_ref, value_ref)[which]
        target = (queries, keys, values)[which]
        columns = pl.ds(pl.multiple_of(head * size, size), size)
        return pltpu.make_async_copy(
            source.at[:, columns], target.at[head], load_sem.at[which, head]
        )

    def store(head):
        columns = pl.ds(pl.multiple_of(head * size, size), size)
        return pltpu.make_async_copy(
            results.at[head], out_ref.at[:, columns], store_sem.at[head]
        )

    @pl.loop(0, heads)
    def _(head):
        for which in range(3):
            load(which, head).start()

    positions = (
        (block_index - SPAN) * rows
        + lax.broadcasted_iota(jnp.int32, doc_rows.shape, 0) * rows
        + lax.broadcasted_iota(jnp.int32, doc_rows.shape, 1)
    )

    def count(doc, carry):
        end, counted = carry
        end = end + lengths_ref[doc]
        return end, counted + jnp.where(positions >= end, 1, 0)

    _, counted = lax.fori_loop(0, doc_total, count, (jnp.int32(0), jnp.zeros_like(positions)))
    inside = (positions >= 0) & (positions < blocks * rows)
    doc_rows[...] = jnp.where(inside, counted, -1).astype(jnp.float32)
    own_docs = jnp.transpose(jnp.broadcast_to(doc_rows[SPAN : SPAN + 1, :], (LANES, rows)))
    for block in range(2 * SPAN + 1):
        for half in range(rows // LANES):
            lanes = slice(half * LANES, (half + 1) * LANES)
            bias[block, :, lanes] = jnp.where(
                own_docs == doc_rows[block : block + 1, lanes], 0.0, MASKED
            )
    edges = (doc_rows[SPAN + 1 : SPAN + 2, 0:1], doc_rows[SPAN - 1 : SPAN, rows - 1 : rows])
    for way in range(2):
        sign = 1 - 2 * way
        for hop in range(SPAN):
            block = SPAN - sign * hop
            select[way, hop] = jnp.where(doc_rows[block : block + 1, :] == edges[way], 1.0, 0.0)

    pl.semaphore_wait(barrier, 2)

    def send(way, hop, slot):
        data = pltpu.make_async_remote_copy(
            src_ref=out_data.at[way, hop, slot],
            dst_ref=in_data.at[way, hop, slot],
            send_sem=data_send.at[way, hop, slot],
            recv_sem=data_recv.at[way, hop, slot],
            device_id=neighbours[way],
            device_id_type=MESH,
        )
        stat = pltpu.make_async_remote_copy(
            src_ref=out_stat.at[way, hop, slot],
            dst_ref=in_stat.at[way, hop, slot],
            send_sem=stat_send.at[way, hop, slot],
            recv_sem=stat_recv.at[way, hop, slot],
            device_id=neighbours[way],
            device_id_type=MESH,
        )
        return stat, data

    def arrive(way, hop, slot):
        for copy in send(way, hop, slot):
            copy.wait_recv()

    def attend(query, head, offset):
        raw = jnp.dot(keys[head], query, preferred_element_type=jnp.float32)
        scores = raw * scaling + bias[SPAN + offset]
        peak = jnp.max(scores, axis=0, keepdims=True)
        weights = jnp.exp(scores - peak)
        total = jnp.sum(weights, axis=0, keepdims=True)
        summed = jnp.dot(
            values_t[head], weights.astype(jnp.bfloat16), preferred_element_type=jnp.float32
        )
        return summed, peak, total

    def arrived(way, hop, slot):
        return in_data[way, hop, slot].astype(jnp.float32), in_stat[way, hop, slot]

    def merge(partial, others):
        summed, peak, total = partial
        top = peak
        for _, level in others:
            top = jnp.maximum(top, level)
        own = jnp.exp(peak - top)
        total = total * own
        shares = [jnp.exp(level - top) for _, level in others]
        for share in shares:
            total = total + share
        inverse = 1.0 / total
        summed = summed * (own * inverse)
        for (data, _), share in zip(others, shares):
            summed = summed + data * (share * inverse)
        return summed, top + jnp.log(total)

    def put(way, hop, slot, query, output, level):
        taken = select[way, hop]
        out_data[way, hop, slot] = jnp.where(
            jnp.broadcast_to(taken, (size, rows)) > 0.5, query.astype(jnp.float32), output
        ).astype(jnp.bfloat16)
        out_stat[way, hop, slot] = jnp.where(taken > 0.5, MASKED, level)

    def post(hop, slot):
        for way in range(2):
            for copy in send(way, hop, slot):
                copy.start()

    def query_of(way, hop, step):
        if hop == 0:
            return queries_t[jnp.minimum(step, heads - 1)]
        return in_data[way, hop - 1, step - hop]

    def pass_on(step, hop, steady):
        slot = step - hop
        head = step - SPAN - 1 - hop

        def partials():
            return [
                attend(
                    in_data[1 - way, SPAN - 1 - hop, head], head, (1 - 2 * way) * (SPAN - hop)
                )
                for way in range(2)
            ]

        def arrivals():
            if hop:
                for way in range(2):
                    arrive(way, hop - 1, slot)

        def outputs(parts):
            for way in range(2):
                others = [arrived(way, hop - 1, slot)] if hop else []
                output, level = merge(parts[way], others)
                put(way, hop, slot, query_of(way, hop, step), output, level)
            post(hop, slot)

        if steady:
            parts = partials()
            arrivals()
            outputs(parts)
            return

        arrivals()

        @pl.when(head >= 0)
        def _():
            outputs(partials())

        @pl.when(head < 0)
        def _():
            for way in range(2):
                put(
                    way,
                    hop,
                    slot,
                    query_of(way, hop, step),
                    jnp.zeros((size, rows), jnp.float32),
                    jnp.full((1, rows), MASKED, jnp.float32),
                )
            post(hop, slot)

    last = slots + SPAN

    def advance(step, steady):
        def guard(condition):
            return (lambda body: body()) if steady else pl.when(condition)

        @guard(step < heads)
        def _():
            load(0, step).wait()
            queries_t[step] = flip(queries[step])

        @guard((step >= SPAN + 1) & (step < SPAN + 1 + heads))
        def _():
            head = step - SPAN - 1
            for which in (1, 2):
                load(which, head).wait()
            values_t[head] = flip(values[head])

        @guard(step >= SPAN + 1)
        def _():
            for way in range(2):
                arrive(way, SPAN - 1, step - SPAN - 1)

        for hop in range(SPAN):

            @guard((step >= hop) & (step < slots + hop))
            def _(hop=hop):
                pass_on(step, hop, steady)

        @guard(step >= 2 * SPAN + 2)
        def _():
            head = step - 2 * SPAN - 2
            partial = attend(queries_t[head], head, 0)
            others = [arrived(way, SPAN - 1, step - SPAN - 1) for way in range(2)]
            output, _ = merge(partial, others)
            results[head] = jnp.transpose(output).astype(jnp.bfloat16)
            store(head).start()

    first = 2 * SPAN + 2

    @pl.loop(0, first)
    def _(step):
        advance(step, False)

    @pl.loop(first, heads)
    def _(step):
        advance(step, True)

    @pl.loop(heads, last + 1)
    def _(step):
        advance(step, False)

    @pl.loop(0, heads)
    def _(head):
        store(head).wait()

    @pl.loop(0, slots)
    def _(slot):
        for way in range(2):
            for hop in range(SPAN):
                for copy in send(way, hop, slot):
                    copy.wait_send()


def on_device(query_states, key_states, value_states, doc_lengths):
    rows, width = query_states.shape
    size = width // HEADS
    slots = HEADS + SPAN + 1
    hbm = pl.BlockSpec(memory_space=pl.ANY)
    mail = pltpu.VMEM((2, SPAN, slots, size, rows), jnp.bfloat16)
    stats = pltpu.VMEM((2, SPAN, slots, 1, rows), jnp.float32)
    held = pltpu.VMEM((HEADS, rows, size), jnp.bfloat16)
    held_t = pltpu.VMEM((HEADS, size, rows), jnp.bfloat16)
    mail_sems = pltpu.SemaphoreType.DMA((2, SPAN, slots))
    return pl.pallas_call(
        functools.partial(kernel, lax.axis_size("outer"), lax.axis_size("inner")),
        out_shape=jax.ShapeDtypeStruct((rows, width), jnp.bfloat16),
        in_specs=[pl.BlockSpec(memory_space=pltpu.SMEM), hbm, hbm, hbm],
        out_specs=hbm,
        scratch_shapes=[
            held,
            held,
            held,
            held,
            mail,
            stats,
            mail,
            stats,
            pltpu.VMEM((2 * SPAN + 1, rows, rows), jnp.float32),
            pltpu.VMEM((SUBLANES, rows), jnp.float32),
            pltpu.VMEM((2, SPAN, 1, rows), jnp.float32),
            held_t,
            held_t,
            pltpu.SemaphoreType.DMA((3, HEADS)),
            pltpu.SemaphoreType.DMA((HEADS,)),
            mail_sems,
            mail_sems,
            mail_sems,
            mail_sems,
        ],
        name="query_mail_attention",
        compiler_params=pltpu.CompilerParams(
            collective_id=0, has_side_effects=True, vmem_limit_bytes=56 * 1024 * 1024
        ),
    )(doc_lengths, query_states, key_states, value_states)


def solution(mesh):
    return jax.shard_map(
        on_device,
        mesh=mesh,
        in_specs=(
            P(("outer", "inner"), None),
            P(("outer", "inner"), None),
            P(("outer", "inner"), None),
            P(),
        ),
        out_specs=P(("outer", "inner"), None),
        check_vma=False,
    )
```

time: 231 us -> 208 us (0.900)
  Pallas kernels: 227 us -> 205 us
    pallas_call x1, Pallas kernels: 227 us -> 205 us  [on_device(): pl.pallas_call(functools.partial(kernel, lax.axis_size('outer'), lax.axis...]
where the time goes in v3:
time: 208 us
  Pallas kernels  205 us (99%)
  local copies, waits for them, and re-layouts  3.13 us (2%)
    pallas_call x1, Pallas kernels, on_device(): pl.pallas_call(functools.partial(kernel, lax.axis_size('outer'), lax.axis...  205 us

profile of v3, /device:TPU:0, one launch (start us, length us, event | category | flops | bytes accessed | tf_op | source)
XLA Modules:
  0.0 208.3 jit_solution(3868690162146435204)
XLA Ops:
  0.0 205.2 %query_mail_attention.1 = bf16[256,4096]{1,0:T(8,128)(2,1)} custom-call(s32[128]{0:T(128)} %lengths_ref.1, bf16[256,4096]{1,0:T(8,128)(2,1)} %query_ref.1, bf16[256,4096]{1,0:T(8,128)(2,1)} %key_ref.1, bf16[256,4096]{1,0:T(8,128)(2,1)} %value_ref.1), custom_call_target="tpu_custom_call" | custom-call | tf_op jit(solution)/shard_map/query_mail_attention/pallas_call | solution.py:312
  205.2 3.1 %copy.6 = bf16[256,4096]{1,0:T(8,128)(2,1)} copy(bf16[256,4096]{1,0:T(8,128)(2,1)} %query_mail_attention.1) | data formatting | bytes 4194304

commit v4 on v1

--- a/solution.py
+++ b/solution.py
@@ -239,9 +239,10 @@
             for which in (0, 1):
                 halo_copy(which, head, up).wait_recv()
 
-        @pl.loop(1, RING)
-        def _(offset):
-            target = ring_place(offset)
+        @pl.loop(0, RING - 1)
+        def _(turn):
+            half = lax.div(turn + 1, 2)
+            target = ring_place(RING // 2 + half * (1 - 2 * lax.rem(turn, 2)))
             attend(head, target)
             result_copy(head, target).start()
 

time: 197 us -> 197 us (level)
  no operation moved by 1% of the time
where the time goes in v4:
time: 197 us; the launch traced here: 195 us
  Pallas kernels  191 us (97%)
  local copies, waits for them, and re-layouts  3.57 us (2%)
    pallas_call x1, Pallas kernels, on_device(): pl.pallas_call(functools.partial(kernel, outer_size, inner_size), out_sha...  191 us

profile of v4, /device:TPU:0, one launch (start us, length us, event | category | flops | bytes accessed | tf_op | source)
XLA Modules:
  0.0 194.7 jit_solution(15347015856517281664)
XLA Ops:
  0.0 0.0 copy-start
  0.0 1.6 copy-done
  1.6 0.0 copy-start.1
  1.6 0.7 copy-done.1
  2.2 191.1 %ring_heads_attention.1 = bf16[256,4096]{1,0:T(8,128)(2,1)S(1)} custom-call(s32[128]{0:T(128)S(1)} %copy-done.1, bf16[256,4096]{1,0:T(8,128)(2,1)S(1)} %copy-done, bf16[256,4096]{1,0:T(8,128)(2,1)} %key_ref.1, bf16[256,4096]{1,0:T(8,128)(2,1)} %value_ref.1), custom_call_target="tpu_custom_call" | custom-call | tf_op jit(solution)/shard_map/ring_heads_attention/pallas_call | solution.py:287
  193.4 1.3 copy.6
Async XLA Ops:
  0.0 1.6 copy-start
  1.6 0.7 copy-start.1
